TPU v7x, 32 devices: a whole 2x2x4 slice. The times are simulated.
32 devices in a mesh: rep: 4 (over y, core), tp: 8 (over z, x).
Axes of the slice: x: 2, y: 2, z: 4, core: 2. Of those that a mesh axis runs over, the one named last changes fastest.
Arguments:
- inputs: bfloat16 [16384, 1024], P(('rep', 'tp')), may hold values from -6 to 6
- cotangent: bfloat16 [16384, 8192], P('rep', 'tp'), may hold values from -1 to 1
- master: float32 [1024, 8192], P('rep', 'tp'), may hold values from -6 to 6
- moment: float32 [1024, 8192], P('rep', 'tp'), may hold values from -6 to 6
- second: float32 [1024, 8192], P('rep', 'tp'), may hold values from 0.5 to 4
Outputs:
- combined: float32 [1024, 8192], P('rep', 'tp')
- moment_new: float32 [1024, 8192], P('rep', 'tp')
- second_new: float32 [1024, 8192], P('rep', 'tp')
- master_new: float32 [1024, 8192], P('rep', 'tp')
- weights: bfloat16 [1024, 8192], P(None, 'tp')
All inputs are finite; a program needn't handle non-finite values.
Results may differ from a plain program's by a relative error of at most 0.001.
Values may be sent and summed in bfloat16 or wider, within the bound.
A program may use at most 64 MiB of HBM per device.

v0:
```python
import functools
import jax
import jax.numpy as jnp
from jax import lax
from jax.experimental import pallas as pl
from jax.experimental.pallas import tpu as pltpu
from jax.sharding import PartitionSpec as P

EPS_SUM = 1e-06
BETA_ONE = 0.9
BETA_TWO = 0.999
LEARN = 0.01
CORRECT_ONE = 1.0 - 0.9**50
CORRECT_TWO = 1.0 - 0.999**50
LANES = 128
SUBLANES = 8
PIECES = 4
SPLIT = 2
OWN_LEAD = 9
LINE_LEAD = 6
INNER_FIRST = 5
MESH = pl.DeviceIdType.MESH


def adasum_weights(gram, replicas):
    entries = [{s: jnp.ones((1, 1), jnp.float32)} for s in range(replicas)]

    def inner(left, right):
        total = None
        for i, u in left.items():
            for j, v in right.items():
                term = (u * v) * gram[min(i, j), max(i, j)]
                total = term if total is None else total + term
        return total

    while len(entries) > 1:
        half = len(entries) // 2
        merged = []
        for a, b in zip(entries[:half], entries[half:]):
            aa, bb, ab = inner(a, a), inner(b, b), inner(a, b)
            ca = 1.0 - ab / (2.0 * (aa + EPS_SUM))
            cb = 1.0 - ab / (2.0 * (bb + EPS_SUM))
            merged.append({**{i: ca * u for i, u in a.items()}, **{i: cb * u for i, u in b.items()}})
        entries = merged
    return entries[0]


def kernel(
    replicas, outer, inner,
    x_hbm, g_hbm, master_hbm, moment_hbm, second_hbm,
    comb_hbm, mom_hbm, sec_hbm, mas_hbm, w_hbm,
    xg, cot, gsend, gr, master, moment, second, comb, mom, sec, mas, wb, tile_tp, tile_rep,
    load_x, load_g, load_s, x_send, x_recv, g_send, g_recv, t_send, t_recv, r_send, r_recv, w_send, w_recv, out_sem,
):
    rep = lax.axis_index("rep")
    tp = lax.axis_index("tp")
    peers = outer * inner
    i, j = tp // inner, tp % inner
    units = xg.shape[0]
    width = xg.shape[3]
    tokens = xg.shape[2]
    chunks = units // SPLIT
    per_segment = chunks // replicas
    segment_order = list(range(replicas - 1, -1, -1))
    rows = gr.shape[1]

    loads = []
    for k in range(units):
        c, part = k // SPLIT, k % SPLIT
        s, h = segment_order[c // per_segment], c % per_segment
        column = pl.multiple_of(((rep ^ s) * per_segment + h) * width, width)
        source = x_hbm.at[pl.ds(part * tokens, tokens), pl.ds(column, width)]
        loads.append(pltpu.make_async_copy(source, xg.at[k, tp], load_x.at[k]))
    for copy in loads:
        copy.start()
    cot_loads = []
    for part in range(SPLIT):
        for slot in range(peers):
            source = g_hbm.at[pl.ds((slot * SPLIT + part) * tokens, tokens)]
            cot_loads.append(pltpu.make_async_copy(source, cot.at[part, pl.ds(slot * tokens, tokens)], load_g.at[part, slot]))
    for copy in cot_loads:
        copy.start()
    state_loads = [
        pltpu.make_async_copy(src, dst, load_s.at[n])
        for n, (src, dst) in enumerate(((master_hbm, master), (moment_hbm, moment), (second_hbm, second)))
    ]
    for copy in state_loads:
        copy.start()

    barrier = pltpu.get_barrier_semaphore()
    for d in range(1, peers):
        pl.semaphore_signal(barrier, inc=1, device_id=(rep, (tp + d) % peers), device_id_type=MESH)
    for s in range(1, replicas):
        pl.semaphore_signal(barrier, inc=1, device_id=(rep ^ s, tp), device_id_type=MESH)
    pl.semaphore_wait(barrier, peers - 1 + replicas - 1)

    pending = []

    def send(k, slot, direction, cond, to_i, to_j):
        target = jnp.clip(to_i, 0, outer - 1) * inner + jnp.clip(to_j, 0, inner - 1)
        copy = pltpu.make_async_remote_copy(
            xg.at[k, slot], xg.at[k, slot], x_send.at[k, direction, slot], x_recv.at[k, slot],
            device_id=(rep, target), device_id_type=MESH,
        )

        @pl.when(cond)
        def _():
            copy.start()

        pending.append((cond, copy))

    def wait_block(k, slot):
        pltpu.make_async_remote_copy(
            xg.at[k, slot], xg.at[k, slot], x_send.at[k, 0, slot], x_recv.at[k, slot],
            device_id=(rep, tp), device_id_type=MESH,
        ).wait_recv()

    def route(k):
        swap = k % INNER_FIRST == 1
        if swap:
            n1, n2, p1, p2 = inner, outer, j, i
            slot_of = lambda q1, q2: q2 * inner + q1
            place = lambda q1, q2: (q2, q1)
        else:
            n1, n2, p1, p2 = outer, inner, i, j
            slot_of = lambda q1, q2: q1 * inner + q2
            place = lambda q1, q2: (q1, q2)
        return n1, n2, p1, p2, slot_of, place

    def cross(k, slot, cond, n2, p1, p2, place):
        up = p2 + 1 < n2
        down = p2 - 1 >= 0
        if cond is not None:
            up, down = cond & up, cond & down
        send(k, slot, 2, up, *place(p1, p2 + 1))
        send(k, slot, 3, down, *place(p1, p2 - 1))

    def own(k):
        n1, n2, p1, p2, slot_of, place = route(k)
        loads[k].wait()
        send(k, tp, 0, p1 + 1 < n1, *place(p1 + 1, p2))
        send(k, tp, 1, p1 - 1 >= 0, *place(p1 - 1, p2))
        cross(k, tp, None, n2, p1, p2, place)

    def first_line(k):
        n1, n2, p1, p2, slot_of, place = route(k)
        for t in range(1, n1):
            for step in (-1, 1):
                origin = p1 + step * t
                valid = (origin >= 0) & (origin < n1)
                slot = slot_of(jnp.clip(origin, 0, n1 - 1), p2)

                @pl.when(valid)
                def _():
                    wait_block(k, slot)

                onward = p1 - step
                send(k, slot, 0 if step < 0 else 1, valid & (onward >= 0) & (onward < n1), *place(onward, p2))
                cross(k, slot, valid, n2, p1, p2, place)

    def second_line(k):
        n1, n2, p1, p2, slot_of, place = route(k)
        for u in range(1, n2):
            for step in (-1, 1):
                origin = p2 + step * u
                valid = (origin >= 0) & (origin < n2)
                onward = p2 - step
                go = valid & (onward >= 0) & (onward < n2)
                for r in range(n1):
                    slot = slot_of((p1 + r) % n1, jnp.clip(origin, 0, n2 - 1))

                    @pl.when(valid)
                    def _():
                        wait_block(k, slot)

                    if n2 > 2:
                        send(k, slot, 2 if step < 0 else 3, go, *place(p1, onward))

    grad_sends = []

    def consume(k):
        c, part = k // SPLIT, k % SPLIT
        s, h = segment_order[c // per_segment], c % per_segment
        at = pl.ds(h * width, width)
        target = gsend.at[s - 1, at] if s else gr.at[0, at]
        product = lax.dot_general(
            xg[k].reshape(peers * tokens, width), cot[part],
            (((0,), (0,)), ((), ())), preferred_element_type=jnp.float32,
        )
        target[...] = target[...] + product if part else product
        if s and part == SPLIT - 1:
            copy = pltpu.make_async_remote_copy(
                gsend.at[s - 1, at], gr.at[s, at], g_send.at[s - 1, h], g_recv.at[s - 1, h],
                device_id=(rep ^ s, tp), device_id_type=MESH,
            )
            copy.start()
            grad_sends.append((h, copy))

    pairs = [(s, t) for s in range(replicas) for t in range(s, replicas)]
    fold = gr.shape[2] // LANES

    def inner_products(h, sums):
        for at_h, copy in grad_sends:
            if at_h == h:
                copy.wait_recv()

        def products(n, sums):
            at = pl.ds(pl.multiple_of(h * width + n * SUBLANES, SUBLANES), SUBLANES)
            block = [gr[s, at, :] for s in range(replicas)]
            out = []
            for total, (s, t) in zip(sums, pairs):
                prod = block[s] * block[t]
                part = prod[:, :LANES]
                for f in range(1, fold):
                    part = part + prod[:, f * LANES : (f + 1) * LANES]
                out.append(total + part)
            return tuple(out)

        return lax.fori_loop(0, width // SUBLANES, products, sums)

    sums = tuple(jnp.zeros((SUBLANES, LANES), jnp.float32) for _ in pairs)
    for k in range(min(OWN_LEAD, units)):
        own(k)
    for k in range(min(LINE_LEAD, units)):
        first_line(k)
    for copy in cot_loads:
        copy.wait()
    for k in range(units):
        if k + OWN_LEAD < units:
            own(k + OWN_LEAD)
        if k + LINE_LEAD < units:
            first_line(k + LINE_LEAD)
        second_line(k)
        if k == units - 1:
            for h in range(per_segment - 1):
                sums = inner_products(h, sums)
        consume(k)
    sums = inner_products(per_segment - 1, sums)
    seg_sends = [copy for _, copy in grad_sends]
    lane = lax.broadcasted_iota(jnp.int32, (SUBLANES, LANES), 1)
    packed = jnp.zeros((SUBLANES, LANES), jnp.float32)
    for n, total in enumerate(sums):
        packed = jnp.where(lane == n, jnp.sum(total, axis=1, keepdims=True), packed)
    tile_tp[0] = packed
    tile_sends = []
    for d in range(1, peers):
        copy = pltpu.make_async_remote_copy(
            tile_tp.at[0], tile_tp.at[d], t_send.at[d - 1], t_recv.at[d - 1],
            device_id=(rep, (tp + d) % peers), device_id_type=MESH,
        )
        copy.start()
        tile_sends.append(copy)
    for copy in state_loads:
        copy.wait()
    for copy in tile_sends:
        copy.wait_recv()
    packed = tile_tp[0]
    for d in range(1, peers):
        packed = packed + tile_tp[d]
    tile_rep[0] = packed
    for s in range(1, replicas):
        copy = pltpu.make_async_remote_copy(
            tile_rep.at[0], tile_rep.at[s], r_send.at[s - 1], r_recv.at[s - 1],
            device_id=(rep ^ s, tp), device_id_type=MESH,
        )
        copy.start()
        tile_sends.append(copy)
    for copy in tile_sends[peers - 1 :]:
        copy.wait_recv()
    index = {pair: n for n, pair in enumerate(pairs)}
    seen = [tile_rep[s] for s in range(replicas)]
    gram = {}
    for s, t in pairs:
        value = None
        for d in range(replicas):
            p, q = s ^ d, t ^ d
            picked = jnp.where(lane == index[min(p, q), max(p, q)], seen[d], 0.0)
            value = picked if value is None else value + picked
        gram[s, t] = jnp.sum(value, keepdims=True)
    coef = adasum_weights(gram, replicas)
    coef = [jnp.broadcast_to(coef[s], (SUBLANES, gr.shape[2])) for s in range(replicas)]

    masks = []
    mask = replicas // 2
    while mask:
        masks.append(mask)
        mask //= 2
    piece = rows // PIECES
    outs = []
    w_copies = {}

    def w_send_start(step, s, q):
        m = masks[step]
        at = pl.ds(q * piece, piece)
        copy = pltpu.make_async_remote_copy(
            wb.at[s, at], wb.at[s ^ m, at], w_send.at[s ^ m, q], w_recv.at[s ^ m, q],
            device_id=(rep ^ m, tp), device_id_type=MESH,
        )
        copy.start()
        w_copies[s ^ m, q] = copy

    def put(src, dst, n):
        copy = pltpu.make_async_copy(src, dst, out_sem.at[n])
        copy.start()
        outs.append(copy)

    for q in range(PIECES):
        def update(n, carry):
            at = pl.ds(pl.multiple_of(q * piece + n * SUBLANES * 2, SUBLANES * 2), SUBLANES * 2)
            value = None
            for s in range(replicas):
                term = coef[s][:1] * gr[s, at, :]
                value = term if value is None else value + term
            moment_new = BETA_ONE * moment[at, :] + (1.0 - BETA_ONE) * value
            second_new = BETA_TWO * second[at, :] + (1.0 - BETA_TWO) * value * value
            master_new = master[at, :] - LEARN * (moment_new / CORRECT_ONE) / (
                jnp.sqrt(second_new / CORRECT_TWO) + 1e-08
            )
            comb[at, :] = value
            mom[at, :] = moment_new
            sec[at, :] = second_new
            mas[at, :] = master_new
            wb[0, at, :] = master_new.astype(jnp.bfloat16)
            return carry

        lax.fori_loop(0, piece // (SUBLANES * 2), update, 0)
        for step in range(len(masks)):
            w_send_start(step, 0, q)
    for n, (src, dst) in enumerate(((comb, comb_hbm), (mom, mom_hbm), (sec, sec_hbm), (mas, mas_hbm))):
        put(src, dst, n)
    put(wb.at[0], w_hbm.at[pl.ds(pl.multiple_of(rep * rows, rows), rows)], 4)

    def relay(q, step, s):
        w_copies[s, q].wait_recv()
        for later in range(step + 1, len(masks)):
            w_send_start(later, s, q)

    held = [0]
    for step, m in enumerate(masks):
        fresh = [s ^ m for s in held]
        for q in range(PIECES):
            for s in fresh:
                relay(q, step, s)
        for s in fresh:
            put(wb.at[s], w_hbm.at[pl.ds(pl.multiple_of((rep ^ s) * rows, rows), rows)], 4 + s)
        held = held + fresh

    for cond, copy in pending:
        @pl.when(cond)
        def _():
            copy.wait_send()
    for copy in seg_sends + tile_sends + list(w_copies.values()):
        copy.wait_send()
    for copy in outs:
        copy.wait()


def deliver(*refs):
    sources, targets, buffers, (in_sem, out_sem) = refs[:5], refs[5:10], refs[10:15], refs[15:]
    moves = []
    for n, (src, dst, buf) in enumerate(zip(sources, targets, buffers)):
        step = buf.shape[0] // PIECES
        for q in range(PIECES):
            at = pl.ds(q * step, step)
            load = pltpu.make_async_copy(src.at[at], buf.at[at], in_sem.at[n, q])
            load.start()
            moves.append((load, pltpu.make_async_copy(buf.at[at], dst.at[at], out_sem.at[n, q])))
    for load, store in moves:
        load.wait()
        store.start()
    for _, store in moves:
        store.wait()


def per_device(inputs, cotangent, master, moment, second):
    replicas = lax.axis_size("rep")
    peers = lax.axis_size("tp")
    inner = 1 << (peers.bit_length() - 1) // 2
    outer = peers // inner
    tokens, depth = inputs.shape
    features = cotangent.shape[1]
    rows = depth // replicas
    width = min(LANES, rows)
    chunks = depth // width
    per_segment = rows // width
    shard = jax.ShapeDtypeStruct((rows, features), jnp.float32)
    anywhere = pl.BlockSpec(memory_space=pl.ANY)
    dma = pltpu.SemaphoreType.DMA
    small = pltpu.VMEM((rows, features), jnp.float32)
    results = pl.pallas_call(
        functools.partial(kernel, replicas, outer, inner),
        out_shape=(shard, shard, shard, shard, jax.ShapeDtypeStruct((depth, features), jnp.bfloat16)),
        in_specs=[anywhere] * 5,
        out_specs=(anywhere,) * 5,
        scratch_shapes=[
            pltpu.VMEM((chunks * SPLIT, peers, tokens // SPLIT, width), jnp.bfloat16),
            pltpu.VMEM((SPLIT, cotangent.shape[0] // SPLIT, features), jnp.bfloat16),
            pltpu.VMEM((replicas - 1, rows, features), jnp.float32),
            pltpu.VMEM((replicas, rows, features), jnp.float32),
            small, small, small, small, small, small, small,
            pltpu.VMEM((replicas, rows, features), jnp.bfloat16),
            pltpu.VMEM((peers, SUBLANES, LANES), jnp.float32),
            pltpu.VMEM((replicas, SUBLANES, LANES), jnp.float32),
            dma((chunks * SPLIT,)),
            dma((SPLIT, peers)),
            dma((3,)),
            dma((chunks * SPLIT, 4, peers)),
            dma((chunks * SPLIT, peers)),
            dma((replicas - 1, per_segment)),
            dma((replicas - 1, per_segment)),
            dma((peers - 1,)),
            dma((peers - 1,)),
            dma((replicas - 1,)),
            dma((replicas - 1,)),
            dma((replicas, PIECES)),
            dma((replicas, PIECES)),
            dma((4 + replicas,)),
        ],
        compiler_params=pltpu.CompilerParams(
            collective_id=0, has_side_effects=True, vmem_limit_bytes=60 * 1024 * 1024
        ),
        name="adasum_adam",
    )(inputs, cotangent, master, moment, second)
    return pl.pallas_call(
        deliver,
        out_shape=tuple(jax.ShapeDtypeStruct(r.shape, r.dtype) for r in results),
        in_specs=[anywhere] * 5,
        out_specs=(anywhere,) * 5,
        scratch_shapes=[pltpu.VMEM(r.shape, r.dtype) for r in results] + [dma((5, PIECES)), dma((5, PIECES))],
        compiler_params=pltpu.CompilerParams(vmem_limit_bytes=60 * 1024 * 1024),
        name="deliver",
    )(*results)


def solution(mesh):
    return jax.shard_map(
        per_device,
        mesh=mesh,
        in_specs=(
            P(("rep", "tp"), None),
            P("rep", "tp"),
            P("rep", "tp"),
            P("rep", "tp"),
            P("rep", "tp"),
        ),
        out_specs=(P("rep", "tp"), P("rep", "tp"), P("rep", "tp"), P("rep", "tp"), P(None, "tp")),
        check_vma=False,
    )
```

profile of v0, /device:TPU:0, one launch (start us, length us, event | category | flops | bytes accessed | tf_op | source)
XLA Modules:
  0.0 134.0 jit_solution(2541834103547685560)
XLA Ops:
  0.6 127.7 %adasum_adam.1 = (f32[256,1024]{1,0:T(8,128)}, f32[256,1024]{1,0:T(8,128)}, f32[256,1024]{1,0:T(8,128)}, f32[256,1024]{1,0:T(8,128)}, bf16[1024,1024]{1,0:T(8,128)(2,1)}) custom-call(bf16[512,1024]{1,0:T(8,128)(2,1)} %x_hbm.1, bf16[4096,1024]{1,0:T(8,128)(2,1)} %g_hbm.1, f32[256,1024]{1,0:T(8,128)} %master_hbm.1, f32[256,1024]{1,0:T(8,128)} %moment_hbm.1, ...), custom_call_target="tpu_custom_call" | custom-call | tf_op jit(solution)/shard_map/adasum_adam/pallas_call | solution.py:390
  128.4 5.4 %deliver.1 = (f32[256,1024]{1,0:T(8,128)}, f32[256,1024]{1,0:T(8,128)}, f32[256,1024]{1,0:T(8,128)}, f32[256,1024]{1,0:T(8,128)}, bf16[1024,1024]{1,0:T(8,128)(2,1)}) custom-call(f32[256,1024]{1,0:T(8,128)} %get-tuple-element.10.refs_0_, f32[256,1024]{1,0:T(8,128)} %get-tuple-element.11.refs_1_, f32[256,1024]{1,0:T(8,128)} %get-tuple-element.12.refs_2_, ...), custom_call_target="tpu_custom_call" | custom-call | tf_op jit(solution)/shard_map/deliver/pallas_call | solution.py:424
where the time goes:
time: 135 us; the launch traced here: 134 us
  Pallas kernels  133 us (99%)
    pallas_call x1, Pallas kernels, per_device(): pl.pallas_call(functools.partial(kernel, replicas, outer, inner), out_sha...  128 us
    pallas_call x1, Pallas kernels, per_device(): pl.pallas_call(deliver, out_shape=tuple((jax.ShapeDtypeStruct(r.shape, r....  5.44 us

commit v1 on v0

v1 whole, which is shorter than its diff:
```python
import functools
import jax
import jax.numpy as jnp
from jax import lax
from jax.experimental import pallas as pl
from jax.experimental.pallas import tpu as pltpu
from jax.sharding import PartitionSpec as P

EPS_SUM = 1e-06
BETA_ONE = 0.9
BETA_TWO = 0.999
LEARN = 0.01
CORRECT_ONE = 1.0 - 0.9**50
CORRECT_TWO = 1.0 - 0.999**50
LANES = 128
SUBLANES = 8
PIECES = 4
SPLIT = 2
OWN_LEAD = 12
LINE_LEAD = (7, 4.5, 3)
SWAP_LEAD = (10,)
LINE_CROSS = (0.5,)
SWAP_CROSS = (0.5, 5, 3)
SWAPPED = (0, 10, 15)
MESH = pl.DeviceIdType.MESH


def adasum_weights(gram, replicas):
    entries = [{s: jnp.ones((1, 1), jnp.float32)} for s in range(replicas)]

    def inner(left, right):
        total = None
        for i, u in left.items():
            for j, v in right.items():
                term = (u * v) * gram[min(i, j), max(i, j)]
                total = term if total is None else total + term
        return total

    while len(entries) > 1:
        half = len(entries) // 2
        merged = []
        for a, b in zip(entries[:half], entries[half:]):
            aa, bb, ab = inner(a, a), inner(b, b), inner(a, b)
            ca = 1.0 - ab / (2.0 * (aa + EPS_SUM))
            cb = 1.0 - ab / (2.0 * (bb + EPS_SUM))
            merged.append({**{i: ca * u for i, u in a.items()}, **{i: cb * u for i, u in b.items()}})
        entries = merged
    return entries[0]


def timeline(units, outer, inner):
    steps = []
    for k in range(units):
        swap = k in SWAPPED
        n1, n2 = (inner, outer) if swap else (outer, inner)
        steps.append((k - OWN_LEAD, 0, "own", k, 0))
        lead = SWAP_LEAD if swap else LINE_LEAD
        late = k - OWN_LEAD
        for t in range(1, n1):
            late = max(late, k - lead[min(t, len(lead)) - 1])
            steps.append((late, t, "line", k, t))
        lead = SWAP_CROSS if swap else LINE_CROSS
        for u in range(1, n2):
            late = max(late, k - lead[min(u, len(lead)) - 1])
            steps.append((late, n1 + u, "cross", k, u))
        steps.append((max(late, k), n1 + n2, "consume", k, 0))
    return [step[2:] for step in sorted(steps)]


def kernel(
    replicas, outer, inner,
    x_hbm, g_hbm, master_hbm, moment_hbm, second_hbm,
    comb, mom, sec, mas, w_out,
    xg, cot, gsend, gr, master, moment, second, tile_tp, tile_rep,
    load_x, load_g, load_s, x_send, x_recv, g_send, g_recv, t_send, t_recv, r_send, r_recv, w_send, w_recv,
):
    rep = lax.axis_index("rep")
    tp = lax.axis_index("tp")
    peers = outer * inner
    i, j = tp // inner, tp % inner
    units = xg.shape[0] // peers
    tokens, width = xg.shape[1], xg.shape[2]
    chunks = units // SPLIT
    per_segment = chunks // replicas
    segment_order = list(range(replicas - 1, -1, -1))
    rows = gr.shape[1]

    loads = []
    for k in range(units):
        c, part = k // SPLIT, k % SPLIT
        s, h = segment_order[c // per_segment], c % per_segment
        column = pl.multiple_of(((rep ^ s) * per_segment + h) * width, width)
        source = x_hbm.at[pl.ds(part * tokens, tokens), pl.ds(column, width)]
        loads.append(pltpu.make_async_copy(source, xg.at[k * peers + tp], load_x.at[k]))
    for copy in loads:
        copy.start()

    barrier = pltpu.get_barrier_semaphore()
    greeted = replicas - 1
    for ok, to_i, to_j in ((i > 0, i - 1, j), (i + 1 < outer, i + 1, j), (j > 0, i, j - 1), (j + 1 < inner, i, j + 1)):
        target = jnp.clip(to_i, 0, outer - 1) * inner + jnp.clip(to_j, 0, inner - 1)

        @pl.when(ok)
        def _():
            pl.semaphore_signal(barrier, inc=1, device_id=(rep, target), device_id_type=MESH)

        greeted = greeted + jnp.where(ok, 1, 0)
    for s in range(1, replicas):
        pl.semaphore_signal(barrier, inc=1, device_id=(rep ^ s, tp), device_id_type=MESH)

    for part in range(SPLIT):
        for slot in range(peers):
            source = g_hbm.at[pl.ds((slot * SPLIT + part) * tokens, tokens)]
            pltpu.make_async_copy(source, cot.at[part, pl.ds(slot * tokens, tokens)], load_g).start()
    state_loads = [
        pltpu.make_async_copy(src, dst, load_s.at[n])
        for n, (src, dst) in enumerate(((master_hbm, master), (moment_hbm, moment), (second_hbm, second)))
    ]
    for copy in state_loads:
        copy.start()
    pl.semaphore_wait(barrier, greeted)

    def send(k, slot, mark, cond, to_i, to_j):
        target = jnp.clip(to_i, 0, outer - 1) * inner + jnp.clip(to_j, 0, inner - 1)
        block = xg.at[k * peers + slot]

        @pl.when(cond)
        def _():
            pltpu.make_async_remote_copy(
                block, block, x_send.at[k], x_recv.at[k, mark], device_id=(rep, target), device_id_type=MESH
            ).start()

    def wait_blocks(k, mark, count, cond):
        block = xg.at[pl.ds(k * peers, count)]

        @pl.when(cond)
        def _():
            pltpu.make_async_remote_copy(
                block, block, x_send.at[k], x_recv.at[k, mark], device_id=(rep, tp), device_id_type=MESH
            ).wait_recv()

    def route(k):
        if k in SWAPPED:
            return inner, outer, j, i, lambda q1, q2: q2 * inner + q1, lambda q1, q2: (q2, q1)
        return outer, inner, i, j, lambda q1, q2: q1 * inner + q2, lambda q1, q2: (q1, q2)

    def cross(k, slot, cond):
        n1, n2, p1, p2, slot_of, place = route(k)
        send(k, slot, n1 + p2, cond & (p2 + 1 < n2), *place(p1, p2 + 1))
        send(k, slot, n1 + p2, cond & (p2 - 1 >= 0), *place(p1, p2 - 1))

    def own(k):
        n1, n2, p1, p2, slot_of, place = route(k)
        loads[k].wait()
        send(k, tp, p1, p1 + 1 < n1, *place(p1 + 1, p2))
        send(k, tp, p1, p1 - 1 >= 0, *place(p1 - 1, p2))
        cross(k, tp, p1 >= 0)

    def line(k, t):
        n1, n2, p1, p2, slot_of, place = route(k)
        for step in (-1, 1):
            origin = p1 + step * t
            valid = (origin >= 0) & (origin < n1)
            origin = jnp.clip(origin, 0, n1 - 1)
            slot = slot_of(origin, p2)
            wait_blocks(k, origin, 1, valid)
            onward = p1 - step
            send(k, slot, origin, valid & (onward >= 0) & (onward < n1), *place(onward, p2))
            cross(k, slot, valid)

    def second_line(k, u):
        n1, n2, p1, p2, slot_of, place = route(k)
        for step in (-1, 1):
            origin = p2 + step * u
            valid = (origin >= 0) & (origin < n2)
            origin = jnp.clip(origin, 0, n2 - 1)
            wait_blocks(k, n1 + origin, n1, valid)
            onward = p2 - step
            if n2 > 2:
                for r in range(n1):
                    slot = slot_of((p1 + r) % n1, origin)
                    send(k, slot, n1 + origin, valid & (onward >= 0) & (onward < n2), *place(p1, onward))

    def drain(at_i, at_j):
        for k in range(units):
            n1, n2, p1, p2 = (inner, outer, at_j, at_i) if k in SWAPPED else (outer, inner, at_i, at_j)
            count = n1 * ((p2 + 1 < n2) + (p2 > 0))
            count += (1 + p1) * (p1 + 1 < n1) + (n1 - p1) * (p1 > 0)
            count += n1 * (p2 * (p2 + 1 < n2) + (n2 - 1 - p2) * (p2 > 0))
            block = xg.at[pl.ds(0, count)]
            pltpu.make_async_remote_copy(
                block, block, x_send.at[k], x_recv.at[k, 0], device_id=(rep, tp), device_id_type=MESH
            ).wait_send()

    grad_sends = []

    def consume(k):
        c, part = k // SPLIT, k % SPLIT
        s, h = segment_order[c // per_segment], c % per_segment
        at = pl.ds(h * width, width)
        target = gsend.at[s - 1, at] if s else gr.at[0, at]
        product = lax.dot_general(
            xg[pl.ds(k * peers, peers)].reshape(peers * tokens, width), cot[part],
            (((0,), (0,)), ((), ())), preferred_element_type=jnp.float32,
        )
        target[...] = target[...] + product if part else product
        if s and part == SPLIT - 1:
            copy = pltpu.make_async_remote_copy(
                gsend.at[s - 1, at], gr.at[s, at], g_send.at[s - 1, h], g_recv.at[s - 1, h],
                device_id=(rep ^ s, tp), device_id_type=MESH,
            )
            copy.start()
            grad_sends.append((h, copy))

    pairs = [(s, t) for s in range(replicas) for t in range(s, replicas)]
    fold = gr.shape[2] // LANES

    def inner_products(h, sums):
        for at_h, copy in grad_sends:
            if at_h == h:
                copy.wait_recv()

        def products(n, sums):
            at = pl.ds(pl.multiple_of(h * width + n * SUBLANES, SUBLANES), SUBLANES)
            block = [gr[s, at, :] for s in range(replicas)]
            out = []
            for total, (s, t) in zip(sums, pairs):
                prod = block[s] * block[t]
                part = prod[:, :LANES]
                for f in range(1, fold):
                    part = part + prod[:, f * LANES : (f + 1) * LANES]
                out.append(total + part)
            return tuple(out)

        return lax.fori_loop(0, width // SUBLANES, products, sums)

    sums = tuple(jnp.zeros((SUBLANES, LANES), jnp.float32) for _ in pairs)
    loaded = False
    for kind, k, t in timeline(units, outer, inner):
        if kind == "own":
            own(k)
        elif kind == "line":
            line(k, t)
        elif kind == "cross":
            second_line(k, t)
        else:
            if not loaded:
                pltpu.make_async_copy(cot, cot, load_g).wait()
                loaded = True
            consume(k)
            if k == units - SPLIT - 1:
                for h in range(per_segment - 1):
                    sums = inner_products(h, sums)
    sums = inner_products(per_segment - 1, sums)
    seg_sends = [copy for _, copy in grad_sends]
    lane = lax.broadcasted_iota(jnp.int32, (SUBLANES, LANES), 1)
    packed = jnp.zeros((SUBLANES, LANES), jnp.float32)
    for n, total in enumerate(sums):
        packed = jnp.where(lane == n, jnp.sum(total, axis=1, keepdims=True), packed)
    tile_tp[0] = packed
    tile_sends = []
    for d in range(1, peers):
        copy = pltpu.make_async_remote_copy(
            tile_tp.at[0], tile_tp.at[d], t_send.at[d - 1], t_recv.at[d - 1],
            device_id=(rep, (tp + d) % peers), device_id_type=MESH,
        )
        copy.start()
        tile_sends.append(copy)
    for copy in state_loads:
        copy.wait()
    for copy in tile_sends:
        copy.wait_recv()
    packed = tile_tp[0]
    for d in range(1, peers):
        packed = packed + tile_tp[d]
    tile_rep[0] = packed
    for s in range(1, replicas):
        copy = pltpu.make_async_remote_copy(
            tile_rep.at[0], tile_rep.at[s], r_send.at[s - 1], r_recv.at[s - 1],
            device_id=(rep ^ s, tp), device_id_type=MESH,
        )
        copy.start()
        tile_sends.append(copy)
    for copy in tile_sends[peers - 1 :]:
        copy.wait_recv()
    index = {pair: n for n, pair in enumerate(pairs)}
    seen = [tile_rep[s] for s in range(replicas)]
    gram = {}
    for s, t in pairs:
        value = None
        for d in range(replicas):
            p, q = s ^ d, t ^ d
            picked = jnp.where(lane == index[min(p, q), max(p, q)], seen[d], 0.0)
            value = picked if value is None else value + picked
        gram[s, t] = jnp.sum(value, keepdims=True)
    coef = adasum_weights(gram, replicas)
    coef = [jnp.broadcast_to(coef[s], (SUBLANES, gr.shape[2])) for s in range(replicas)]

    masks = []
    mask = replicas // 2
    while mask:
        masks.append(mask)
        mask //= 2
    piece = rows // PIECES
    w_copies = {}

    def w_at(s, q):
        return w_out.at[pl.ds(pl.multiple_of((rep ^ s) * rows + q * piece, piece), piece)]

    def w_send_start(step, s, q):
        m = masks[step]
        copy = pltpu.make_async_remote_copy(
            w_at(s, q), w_at(s, q), w_send.at[s ^ m, q], w_recv.at[s ^ m, q],
            device_id=(rep ^ m, tp), device_id_type=MESH,
        )
        copy.start()
        w_copies[s ^ m, q] = copy

    for q in range(PIECES):
        def update(n, carry):
            at = pl.ds(pl.multiple_of(q * piece + n * SUBLANES * 2, SUBLANES * 2), SUBLANES * 2)
            value = None
            for s in range(replicas):
                term = coef[s][:1] * gr[s, at, :]
                value = term if value is None else value + term
            moment_new = BETA_ONE * moment[at, :] + (1.0 - BETA_ONE) * value
            second_new = BETA_TWO * second[at, :] + (1.0 - BETA_TWO) * value * value
            master_new = master[at, :] - LEARN * (moment_new / CORRECT_ONE) / (
                jnp.sqrt(second_new / CORRECT_TWO) + 1e-08
            )
            comb[at, :] = value
            mom[at, :] = moment_new
            sec[at, :] = second_new
            mas[at, :] = master_new
            own_at = pl.ds(pl.multiple_of(rep * rows + q * piece + n * SUBLANES * 2, SUBLANES * 2), SUBLANES * 2)
            w_out[own_at, :] = master_new.astype(jnp.bfloat16)
            return carry

        lax.fori_loop(0, piece // (SUBLANES * 2), update, 0)
        for step in range(len(masks)):
            w_send_start(step, 0, q)
    def relay(q, step, s):
        w_copies[s, q].wait_recv()
        for later in range(step + 1, len(masks)):
            w_send_start(later, s, q)

    held = [0]
    for step, m in enumerate(masks):
        fresh = [s ^ m for s in held]
        for q in range(PIECES):
            for s in fresh:
                relay(q, step, s)
        held = held + fresh

    for at_i in range(outer):
        for at_j in range(inner):
            pl.when((i == at_i) & (j == at_j))(functools.partial(drain, at_i, at_j))
    for copy in seg_sends + tile_sends + list(w_copies.values()):
        copy.wait_send()


def deliver(*refs):
    sources, targets, sem = refs[:5], refs[5:10], refs[10]
    moves = []
    for n, (src, dst) in enumerate(zip(sources, targets)):
        step = src.shape[0] // PIECES
        for q in range(PIECES):
            at = pl.ds(q * step, step)
            moves.append(pltpu.make_async_copy(src.at[at], dst.at[at], sem.at[n, q]))
            moves[-1].start()
    for move in moves:
        move.wait()


def per_device(inputs, cotangent, master, moment, second):
    replicas = lax.axis_size("rep")
    peers = lax.axis_size("tp")
    inner = 1 << (peers.bit_length() - 1) // 2
    outer = peers // inner
    tokens, depth = inputs.shape
    features = cotangent.shape[1]
    rows = depth // replicas
    width = min(LANES, rows)
    chunks = depth // width
    per_segment = rows // width
    units = chunks * SPLIT
    anywhere = pl.BlockSpec(memory_space=pl.ANY)
    vmem = pl.BlockSpec(memory_space=pltpu.VMEM)
    dma = pltpu.SemaphoreType.DMA
    small = pltpu.VMEM((rows, features), jnp.float32)
    results = pl.pallas_call(
        functools.partial(kernel, replicas, outer, inner),
        out_shape=(small, small, small, small, pltpu.VMEM((depth, features), jnp.bfloat16)),
        in_specs=[anywhere] * 5,
        out_specs=(vmem,) * 5,
        scratch_shapes=[
            pltpu.VMEM((units * peers, tokens // SPLIT, width), jnp.bfloat16),
            pltpu.VMEM((SPLIT, cotangent.shape[0] // SPLIT, features), jnp.bfloat16),
            pltpu.VMEM((replicas - 1, rows, features), jnp.float32),
            pltpu.VMEM((replicas, rows, features), jnp.float32),
            small, small, small,
            pltpu.VMEM((peers, SUBLANES, LANES), jnp.float32),
            pltpu.VMEM((replicas, SUBLANES, LANES), jnp.float32),
            dma((units,)),
            dma(()),
            dma((3,)),
            dma((units,)),
            dma((units, outer + inner)),
            dma((replicas - 1, per_segment)),
            dma((replicas - 1, per_segment)),
            dma((peers - 1,)),
            dma((peers - 1,)),
            dma((replicas - 1,)),
            dma((replicas - 1,)),
            dma((replicas, PIECES)),
            dma((replicas, PIECES)),
        ],
        compiler_params=pltpu.CompilerParams(
            collective_id=0, has_side_effects=True, vmem_limit_bytes=48 * 1024 * 1024
        ),
        name="adasum_adam",
    )(inputs, cotangent, master, moment, second)
    results = [pltpu.with_memory_space_constraint(r, pltpu.VMEM) for r in results]
    return pl.pallas_call(
        deliver,
        out_shape=tuple(jax.ShapeDtypeStruct(r.shape, r.dtype) for r in results),
        in_specs=[vmem] * 5,
        out_specs=(anywhere,) * 5,
        scratch_shapes=[dma((5, PIECES))],
        compiler_params=pltpu.CompilerParams(vmem_limit_bytes=1024 * 1024),
        name="deliver",
    )(*results)


def solution(mesh):
    return jax.shard_map(
        per_device,
        mesh=mesh,
        in_specs=(
            P(("rep", "tp"), None),
            P("rep", "tp"),
            P("rep", "tp"),
            P("rep", "tp"),
            P("rep", "tp"),
        ),
        out_specs=(P("rep", "tp"), P("rep", "tp"), P("rep", "tp"), P("rep", "tp"), P(None, "tp")),
        check_vma=False,
    )
```

time: 135 us -> 120 us (0.89)
  Pallas kernels: 133 us -> 119 us
    pallas_call x1, Pallas kernels: 128 us -> 116 us  [per_device(): pl.pallas_call(functools.partial(kernel, replicas, outer, inner), out_sha...]
    pallas_call x1, Pallas kernels: 5.44 us -> 2.82 us  [per_device(): pl.pallas_call(deliver, out_shape=tuple((jax.ShapeDtypeStruct(r.shape, r....]
where the time goes in v1:
time: 120 us
  Pallas kernels  119 us (99%)
    pallas_call x1, Pallas kernels, per_device(): pl.pallas_call(functools.partial(kernel, replicas, outer, inner), out_sha...  116 us
    pallas_call x1, Pallas kernels, per_device(): pl.pallas_call(deliver, out_shape=tuple((jax.ShapeDtypeStruct(r.shape, r....  2.82 us

profile of v1, /device:TPU:0, one launch (start us, length us, event | category | flops | bytes accessed | tf_op | source)
XLA Modules:
  0.0 120.1 jit_solution(4897736220965852567)
XLA Ops:
  0.6 116.4 %adasum_adam.1 = (f32[256,1024]{1,0:T(8,128)S(1)}, f32[256,1024]{1,0:T(8,128)S(1)}, f32[256,1024]{1,0:T(8,128)S(1)}, f32[256,1024]{1,0:T(8,128)S(1)}, bf16[1024,1024]{1,0:T(8,128)(2,1)S(1)}) custom-call(bf16[512,1024]{1,0:T(8,128)(2,1)} %x_hbm.1, bf16[4096,1024]{1,0:T(8,128)(2,1)} %g_hbm.1, f32[256,1024]{1,0:T(8,128)} %master_hbm.1, f32[256,1024]{1,0:T(8,128)} %moment_hbm.1, ...), custom_call_target="tpu_custom_call" | custom-call | tf_op jit(solution)/shard_map/adasum_adam/pallas_call | solution.py:391
  117.1 2.8 %deliver.1 = (f32[256,1024]{1,0:T(8,128)}, f32[256,1024]{1,0:T(8,128)}, f32[256,1024]{1,0:T(8,128)}, f32[256,1024]{1,0:T(8,128)}, bf16[1024,1024]{1,0:T(8,128)(2,1)}) custom-call(f32[256,1024]{1,0:T(8,128)S(1)} %get-tuple-element.10.refs_0_, f32[256,1024]{1,0:T(8,128)S(1)} %get-tuple-element.11.refs_1_, f32[256,1024]{1,0:T(8,128)S(1)} %get-tuple-element.12.refs_2_, ...), custom_call_target="tpu_custom_call" | custom-call | tf_op jit(solution)/shard_map/deliver/pallas_call | solution.py:424

commit v2 on v1

--- a/solution.py
+++ b/solution.py
@@ -16,12 +16,14 @@
 SUBLANES = 8
 PIECES = 4
 SPLIT = 2
-OWN_LEAD = 12
-LINE_LEAD = (7, 4.5, 3)
-SWAP_LEAD = (10,)
-LINE_CROSS = (0.5,)
-SWAP_CROSS = (0.5, 5, 3)
-SWAPPED = (0, 10, 15)
+OWN_LEAD = 11
+LINE_LEAD = (7, 5.5, 3.5)
+SWAP_LEAD = (6.5,)
+LINE_CROSS = (0,)
+SWAP_CROSS = (3.5, 2.5, 0)
+SWAPPED = (8, 12, 15)
+GROUP = 4
+BATCH = 8
 MESH = pl.DeviceIdType.MESH
 
 
@@ -71,8 +73,8 @@
     replicas, outer, inner,
     x_hbm, g_hbm, master_hbm, moment_hbm, second_hbm,
     comb, mom, sec, mas, w_out,
-    xg, cot, gsend, gr, master, moment, second, tile_tp, tile_rep,
-    load_x, load_g, load_s, x_send, x_recv, g_send, g_recv, t_send, t_recv, r_send, r_recv, w_send, w_recv,
+    xg, cot, gsend, gr, states, tile_tp,
+    load_x, load_g, load_s, x_send, x_recv, g_send, g_recv, t_send, t_recv, w_send, w_recv, w_last,
 ):
     rep = lax.axis_index("rep")
     tp = lax.axis_index("tp")
@@ -85,15 +87,12 @@
     segment_order = list(range(replicas - 1, -1, -1))
     rows = gr.shape[1]
 
-    loads = []
     for k in range(units):
         c, part = k // SPLIT, k % SPLIT
         s, h = segment_order[c // per_segment], c % per_segment
         column = pl.multiple_of(((rep ^ s) * per_segment + h) * width, width)
         source = x_hbm.at[pl.ds(part * tokens, tokens), pl.ds(column, width)]
-        loads.append(pltpu.make_async_copy(source, xg.at[k * peers + tp], load_x.at[k]))
-    for copy in loads:
-        copy.start()
+        pltpu.make_async_copy(source, xg.at[k * peers + tp], load_x.at[k // GROUP]).start()
 
     barrier = pltpu.get_barrier_semaphore()
     greeted = replicas - 1
@@ -112,12 +111,8 @@
         for slot in range(peers):
             source = g_hbm.at[pl.ds((slot * SPLIT + part) * tokens, tokens)]
             pltpu.make_async_copy(source, cot.at[part, pl.ds(slot * tokens, tokens)], load_g).start()
-    state_loads = [
-        pltpu.make_async_copy(src, dst, load_s.at[n])
-        for n, (src, dst) in enumerate(((master_hbm, master), (moment_hbm, moment), (second_hbm, second)))
-    ]
-    for copy in state_loads:
-        copy.start()
+    for n, source in enumerate((master_hbm, moment_hbm, second_hbm)):
+        pltpu.make_async_copy(source, states.at[n], load_s).start()
     pl.semaphore_wait(barrier, greeted)
 
     def send(k, slot, mark, cond, to_i, to_j):
@@ -127,7 +122,7 @@
         @pl.when(cond)
         def _():
             pltpu.make_async_remote_copy(
-                block, block, x_send.at[k], x_recv.at[k, mark], device_id=(rep, target), device_id_type=MESH
+                block, block, x_send.at[k // BATCH], x_recv.at[k, mark], device_id=(rep, target), device_id_type=MESH
             ).start()
 
     def wait_blocks(k, mark, count, cond):
@@ -136,7 +131,7 @@
         @pl.when(cond)
         def _():
             pltpu.make_async_remote_copy(
-                block, block, x_send.at[k], x_recv.at[k, mark], device_id=(rep, tp), device_id_type=MESH
+                block, block, x_send.at[0], x_recv.at[k, mark], device_id=(rep, tp), device_id_type=MESH
             ).wait_recv()
 
     def route(k):
@@ -146,14 +141,16 @@
 
     def cross(k, slot, cond):
         n1, n2, p1, p2, slot_of, place = route(k)
-        send(k, slot, n1 + p2, cond & (p2 + 1 < n2), *place(p1, p2 + 1))
-        send(k, slot, n1 + p2, cond & (p2 - 1 >= 0), *place(p1, p2 - 1))
+        send(k, slot, n1 - 1 + p2, cond & (p2 + 1 < n2), *place(p1, p2 + 1))
+        send(k, slot, n1 - 2 + p2, cond & (p2 - 1 >= 0), *place(p1, p2 - 1))
 
     def own(k):
         n1, n2, p1, p2, slot_of, place = route(k)
-        loads[k].wait()
+        if k % GROUP == 0:
+            block = xg.at[pl.ds(0, min(GROUP, units - k))]
+            pltpu.make_async_copy(block, block, load_x.at[k // GROUP]).wait()
         send(k, tp, p1, p1 + 1 < n1, *place(p1 + 1, p2))
-        send(k, tp, p1, p1 - 1 >= 0, *place(p1 - 1, p2))
+        send(k, tp, p1 - 1, p1 - 1 >= 0, *place(p1 - 1, p2))
         cross(k, tp, p1 >= 0)
 
     def line(k, t):
@@ -163,9 +160,10 @@
             valid = (origin >= 0) & (origin < n1)
             origin = jnp.clip(origin, 0, n1 - 1)
             slot = slot_of(origin, p2)
-            wait_blocks(k, origin, 1, valid)
+            mark = jnp.clip(origin - (step > 0), 0, n1 - 2)
+            wait_blocks(k, mark, 1, valid)
             onward = p1 - step
-            send(k, slot, origin, valid & (onward >= 0) & (onward < n1), *place(onward, p2))
+            send(k, slot, mark, valid & (onward >= 0) & (onward < n1), *place(onward, p2))
             cross(k, slot, valid)
 
     def second_line(k, u):
@@ -174,25 +172,27 @@
             origin = p2 + step * u
             valid = (origin >= 0) & (origin < n2)
             origin = jnp.clip(origin, 0, n2 - 1)
-            wait_blocks(k, n1 + origin, n1, valid)
+            mark = n1 - 1 + jnp.clip(origin - (step > 0), 0, n2 - 2)
+            wait_blocks(k, mark, n1, valid)
             onward = p2 - step
             if n2 > 2:
                 for r in range(n1):
                     slot = slot_of((p1 + r) % n1, origin)
-                    send(k, slot, n1 + origin, valid & (onward >= 0) & (onward < n2), *place(p1, onward))
+                    send(k, slot, mark, valid & (onward >= 0) & (onward < n2), *place(p1, onward))
 
     def drain(at_i, at_j):
+        totals = [0] * -(-units // BATCH)
         for k in range(units):
             n1, n2, p1, p2 = (inner, outer, at_j, at_i) if k in SWAPPED else (outer, inner, at_i, at_j)
             count = n1 * ((p2 + 1 < n2) + (p2 > 0))
             count += (1 + p1) * (p1 + 1 < n1) + (n1 - p1) * (p1 > 0)
             count += n1 * (p2 * (p2 + 1 < n2) + (n2 - 1 - p2) * (p2 > 0))
+            totals[k // BATCH] += count
+        for n, count in enumerate(totals):
             block = xg.at[pl.ds(0, count)]
             pltpu.make_async_remote_copy(
-                block, block, x_send.at[k], x_recv.at[k, 0], device_id=(rep, tp), device_id_type=MESH
+                block, block, x_send.at[n], x_recv.at[0, 0], device_id=(rep, tp), device_id_type=MESH
             ).wait_send()
-
-    grad_sends = []
 
     def consume(k):
         c, part = k // SPLIT, k % SPLIT
@@ -206,19 +206,17 @@
         target[...] = target[...] + product if part else product
         if s and part == SPLIT - 1:
             copy = pltpu.make_async_remote_copy(
-                gsend.at[s - 1, at], gr.at[s, at], g_send.at[s - 1, h], g_recv.at[s - 1, h],
+                gsend.at[s - 1, at], gr.at[s, at], g_send, g_recv.at[h],
                 device_id=(rep ^ s, tp), device_id_type=MESH,
             )
             copy.start()
-            grad_sends.append((h, copy))
 
     pairs = [(s, t) for s in range(replicas) for t in range(s, replicas)]
     fold = gr.shape[2] // LANES
 
     def inner_products(h, sums):
-        for at_h, copy in grad_sends:
-            if at_h == h:
-                copy.wait_recv()
+        piece = gr.at[pl.ds(0, replicas - 1), pl.ds(h * width, width)]
+        pltpu.make_async_copy(piece, piece, g_recv.at[h]).wait()
 
         def products(n, sums):
             at = pl.ds(pl.multiple_of(h * width + n * SUBLANES, SUBLANES), SUBLANES)
@@ -248,43 +246,32 @@
                 pltpu.make_async_copy(cot, cot, load_g).wait()
                 loaded = True
             consume(k)
-            if k == units - SPLIT - 1:
+            if k == units - 2:
                 for h in range(per_segment - 1):
                     sums = inner_products(h, sums)
     sums = inner_products(per_segment - 1, sums)
-    seg_sends = [copy for _, copy in grad_sends]
     lane = lax.broadcasted_iota(jnp.int32, (SUBLANES, LANES), 1)
     packed = jnp.zeros((SUBLANES, LANES), jnp.float32)
     for n, total in enumerate(sums):
         packed = jnp.where(lane == n, jnp.sum(total, axis=1, keepdims=True), packed)
     tile_tp[0] = packed
-    tile_sends = []
-    for d in range(1, peers):
-        copy = pltpu.make_async_remote_copy(
-            tile_tp.at[0], tile_tp.at[d], t_send.at[d - 1], t_recv.at[d - 1],
-            device_id=(rep, (tp + d) % peers), device_id_type=MESH,
-        )
-        copy.start()
-        tile_sends.append(copy)
-    for copy in state_loads:
-        copy.wait()
-    for copy in tile_sends:
-        copy.wait_recv()
-    packed = tile_tp[0]
-    for d in range(1, peers):
-        packed = packed + tile_tp[d]
-    tile_rep[0] = packed
-    for s in range(1, replicas):
-        copy = pltpu.make_async_remote_copy(
-            tile_rep.at[0], tile_rep.at[s], r_send.at[s - 1], r_recv.at[s - 1],
-            device_id=(rep ^ s, tp), device_id_type=MESH,
-        )
-        copy.start()
-        tile_sends.append(copy)
-    for copy in tile_sends[peers - 1 :]:
-        copy.wait_recv()
+    for d in range(peers - 1, -1, -1):
+        for s in range(replicas - 1, -1, -1):
+            if d or s:
+                pltpu.make_async_remote_copy(
+                    tile_tp.at[0], tile_tp.at[s * peers + d], t_send, t_recv,
+                    device_id=(rep ^ s, (tp + d) % peers), device_id_type=MESH,
+                ).start()
+    pltpu.make_async_copy(states, states, load_s).wait()
+    others = tile_tp.at[pl.ds(1, replicas * peers - 1)]
+    pltpu.make_async_copy(others, others, t_recv).wait()
     index = {pair: n for n, pair in enumerate(pairs)}
-    seen = [tile_rep[s] for s in range(replicas)]
+    seen = []
+    for s in range(replicas):
+        total = tile_tp[s * peers]
+        for d in range(1, peers):
+            total = total + tile_tp[s * peers + d]
+        seen.append(total)
     gram = {}
     for s, t in pairs:
         value = None
@@ -302,19 +289,18 @@
         masks.append(mask)
         mask //= 2
     piece = rows // PIECES
-    w_copies = {}
 
     def w_at(s, q):
         return w_out.at[pl.ds(pl.multiple_of((rep ^ s) * rows + q * piece, piece), piece)]
 
+    last = len(masks) - 1
+
     def w_send_start(step, s, q):
         m = masks[step]
-        copy = pltpu.make_async_remote_copy(
-            w_at(s, q), w_at(s, q), w_send.at[s ^ m, q], w_recv.at[s ^ m, q],
+        pltpu.make_async_remote_copy(
+            w_at(s, q), w_at(s, q), w_send, w_last if step == last else w_recv.at[s ^ m, q],
             device_id=(rep ^ m, tp), device_id_type=MESH,
-        )
-        copy.start()
-        w_copies[s ^ m, q] = copy
+        ).start()
 
     for q in range(PIECES):
         def update(n, carry):
@@ -323,9 +309,9 @@
             for s in range(replicas):
                 term = coef[s][:1] * gr[s, at, :]
                 value = term if value is None else value + term
-            moment_new = BETA_ONE * moment[at, :] + (1.0 - BETA_ONE) * value
-            second_new = BETA_TWO * second[at, :] + (1.0 - BETA_TWO) * value * value
-            master_new = master[at, :] - LEARN * (moment_new / CORRECT_ONE) / (
+            moment_new = BETA_ONE * states[1, at, :] + (1.0 - BETA_ONE) * value
+            second_new = BETA_TWO * states[2, at, :] + (1.0 - BETA_TWO) * value * value
+            master_new = states[0, at, :] - LEARN * (moment_new / CORRECT_ONE) / (
                 jnp.sqrt(second_new / CORRECT_TWO) + 1e-08
             )
             comb[at, :] = value
@@ -340,23 +326,27 @@
         for step in range(len(masks)):
             w_send_start(step, 0, q)
     def relay(q, step, s):
-        w_copies[s, q].wait_recv()
+        pltpu.make_async_copy(w_at(s, q), w_at(s, q), w_recv.at[s, q]).wait()
         for later in range(step + 1, len(masks)):
             w_send_start(later, s, q)
 
     held = [0]
-    for step, m in enumerate(masks):
+    for step, m in enumerate(masks[:-1]):
         fresh = [s ^ m for s in held]
         for q in range(PIECES):
             for s in fresh:
                 relay(q, step, s)
         held = held + fresh
 
+    half = w_out.at[pl.ds(0, replicas // 2 * rows)]
+    pltpu.make_async_copy(half, half, w_last).wait()
     for at_i in range(outer):
         for at_j in range(inner):
             pl.when((i == at_i) & (j == at_j))(functools.partial(drain, at_i, at_j))
-    for copy in seg_sends + tile_sends + list(w_copies.values()):
-        copy.wait_send()
+    pltpu.make_async_copy(gsend, gsend, g_send).wait()
+    pltpu.make_async_copy(others, others, t_send).wait()
+    sent = w_out.at[pl.ds(0, (replicas - 1) * rows)]
+    pltpu.make_async_copy(sent, sent, w_send).wait()
 
 
 def deliver(*refs):
@@ -398,22 +388,20 @@
             pltpu.VMEM((SPLIT, cotangent.shape[0] // SPLIT, features), jnp.bfloat16),
             pltpu.VMEM((replicas - 1, rows, features), jnp.float32),
             pltpu.VMEM((replicas, rows, features), jnp.float32),
-            small, small, small,
-            pltpu.VMEM((peers, SUBLANES, LANES), jnp.float32),
-            pltpu.VMEM((replicas, SUBLANES, LANES), jnp.float32),
-            dma((units,)),
-            dma(()),
-            dma((3,)),
-            dma((units,)),
-            dma((units, outer + inner)),
-            dma((replicas - 1, per_segment)),
-            dma((replicas - 1, per_segment)),
-            dma((peers - 1,)),
-            dma((peers - 1,)),
-            dma((replicas - 1,)),
-            dma((replicas - 1,)),
+            pltpu.VMEM((3, rows, features), jnp.float32),
+            pltpu.VMEM((replicas * peers, SUBLANES, LANES), jnp.float32),
+            dma((-(-units // GROUP),)),
+            dma(()),
+            dma(()),
+            dma((-(-units // BATCH),)),
+            dma((units, outer + inner - 2)),
+            dma(()),
+            dma((per_segment,)),
+            dma(()),
+            dma(()),
+            dma(()),
             dma((replicas, PIECES)),
-            dma((replicas, PIECES)),
+            dma(()),
         ],
         compiler_params=pltpu.CompilerParams(
             collective_id=0, has_side_effects=True, vmem_limit_bytes=48 * 1024 * 1024

time: 120 us -> 112 us (0.933)
  Pallas kernels: 119 us -> 112 us
    pallas_call x1, Pallas kernels: 116 us -> 109 us  [per_device(): pl.pallas_call(functools.partial(kernel, replicas, outer, inner), out_sha...]
where the time goes in v2:
time: 112 us
  Pallas kernels  112 us (100%)
    pallas_call x1, Pallas kernels, per_device(): pl.pallas_call(functools.partial(kernel, replicas, outer, inner), out_sha...  109 us
    pallas_call x1, Pallas kernels, per_device(): pl.pallas_call(deliver, out_shape=tuple((jax.ShapeDtypeStruct(r.shape, r....  2.82 us

profile of v2, /device:TPU:0, one launch (start us, length us, event | category | flops | bytes accessed | tf_op | source)
XLA Modules:
  0.0 112.3 jit_solution(143229600651045911)
XLA Ops:
  0.6 108.8 %adasum_adam.1 = (f32[256,1024]{1,0:T(8,128)S(1)}, f32[256,1024]{1,0:T(8,128)S(1)}, f32[256,1024]{1,0:T(8,128)S(1)}, f32[256,1024]{1,0:T(8,128)S(1)}, bf16[1024,1024]{1,0:T(8,128)(2,1)S(1)}) custom-call(bf16[512,1024]{1,0:T(8,128)(2,1)} %x_hbm.1, bf16[4096,1024]{1,0:T(8,128)(2,1)} %g_hbm.1, f32[256,1024]{1,0:T(8,128)} %master_hbm.1, f32[256,1024]{1,0:T(8,128)} %moment_hbm.1, ...), custom_call_target="tpu_custom_call" | custom-call | tf_op jit(solution)/shard_map/adasum_adam/pallas_call | solution.py:381
  109.4 2.8 %deliver.1 = (f32[256,1024]{1,0:T(8,128)}, f32[256,1024]{1,0:T(8,128)}, f32[256,1024]{1,0:T(8,128)}, f32[256,1024]{1,0:T(8,128)}, bf16[1024,1024]{1,0:T(8,128)(2,1)}) custom-call(f32[256,1024]{1,0:T(8,128)S(1)} %get-tuple-element.10.refs_0_, f32[256,1024]{1,0:T(8,128)S(1)} %get-tuple-element.11.refs_1_, f32[256,1024]{1,0:T(8,128)S(1)} %get-tuple-element.12.refs_2_, ...), custom_call_target="tpu_custom_call" | custom-call | tf_op jit(solution)/shard_map/deliver/pallas_call | solution.py:412

commit v3 on v2

--- a/solution.py
+++ b/solution.py
@@ -14,16 +14,17 @@
 CORRECT_TWO = 1.0 - 0.999**50
 LANES = 128
 SUBLANES = 8
-PIECES = 4
+PIECES = 8
 SPLIT = 2
-OWN_LEAD = 11
-LINE_LEAD = (7, 5.5, 3.5)
-SWAP_LEAD = (6.5,)
+OWN_LEAD = 9
+LINE_LEAD = (4.5, 3.5, 2.5)
+SWAP_LEAD = (7.0,)
 LINE_CROSS = (0,)
-SWAP_CROSS = (3.5, 2.5, 0)
-SWAPPED = (8, 12, 15)
+SWAP_CROSS = (4.0, 2.0, 1.5)
+SWAPPED = (5, 14)
 GROUP = 4
 BATCH = 8
+MIXED = 11
 MESH = pl.DeviceIdType.MESH
 
 
@@ -53,7 +54,8 @@
 def timeline(units, outer, inner):
     steps = []
     for k in range(units):
-        swap = k in SWAPPED
+        mixed = k == MIXED and inner == 2
+        swap = not mixed and k in SWAPPED + (MIXED,)
         n1, n2 = (inner, outer) if swap else (outer, inner)
         steps.append((k - OWN_LEAD, 0, "own", k, 0))
         lead = SWAP_LEAD if swap else LINE_LEAD
@@ -61,6 +63,12 @@
         for t in range(1, n1):
             late = max(late, k - lead[min(t, len(lead)) - 1])
             steps.append((late, t, "line", k, t))
+        if mixed:
+            turn = max(k - OWN_LEAD, k - SWAP_LEAD[0])
+            steps.append((turn, 0.5, "turn", k, 0))
+            for u in range(1, n1):
+                turn = max(turn, k - SWAP_CROSS[min(u, len(SWAP_CROSS)) - 1])
+                steps.append((turn, n1 + u, "pass", k, u))
         lead = SWAP_CROSS if swap else LINE_CROSS
         for u in range(1, n2):
             late = max(late, k - lead[min(u, len(lead)) - 1])
@@ -74,7 +82,7 @@
     x_hbm, g_hbm, master_hbm, moment_hbm, second_hbm,
     comb, mom, sec, mas, w_out,
     xg, cot, gsend, gr, states, tile_tp,
-    load_x, load_g, load_s, x_send, x_recv, g_send, g_recv, t_send, t_recv, w_send, w_recv, w_last,
+    load_x, load_g, load_s, x_send, x_recv, m_recv, g_send, g_recv, t_send, t_recv, w_send, w_recv, w_last,
 ):
     rep = lax.axis_index("rep")
     tp = lax.axis_index("tp")
@@ -82,6 +90,9 @@
     i, j = tp // inner, tp % inner
     units = xg.shape[0] // peers
     tokens, width = xg.shape[1], xg.shape[2]
+    swapped = SWAPPED if inner == 2 else SWAPPED + (MIXED,)
+    mixed = MIXED if inner == 2 else units
+    middle = (outer // 2 - 1, outer // 2)
     chunks = units // SPLIT
     per_segment = chunks // replicas
     segment_order = list(range(replicas - 1, -1, -1))
@@ -115,27 +126,27 @@
         pltpu.make_async_copy(source, states.at[n], load_s).start()
     pl.semaphore_wait(barrier, greeted)
 
-    def send(k, slot, mark, cond, to_i, to_j):
+    def send(k, slot, mark, cond, to_i, to_j, arrived=None):
         target = jnp.clip(to_i, 0, outer - 1) * inner + jnp.clip(to_j, 0, inner - 1)
         block = xg.at[k * peers + slot]
 
         @pl.when(cond)
         def _():
             pltpu.make_async_remote_copy(
-                block, block, x_send.at[k // BATCH], x_recv.at[k, mark], device_id=(rep, target), device_id_type=MESH
+                block, block, x_send.at[k // BATCH], x_recv.at[k, mark] if arrived is None else arrived, device_id=(rep, target), device_id_type=MESH
             ).start()
 
-    def wait_blocks(k, mark, count, cond):
+    def wait_blocks(k, mark, count, cond, arrived=None):
         block = xg.at[pl.ds(k * peers, count)]
 
         @pl.when(cond)
         def _():
             pltpu.make_async_remote_copy(
-                block, block, x_send.at[0], x_recv.at[k, mark], device_id=(rep, tp), device_id_type=MESH
+                block, block, x_send.at[0], x_recv.at[k, mark] if arrived is None else arrived, device_id=(rep, tp), device_id_type=MESH
             ).wait_recv()
 
     def route(k):
-        if k in SWAPPED:
+        if k in swapped:
             return inner, outer, j, i, lambda q1, q2: q2 * inner + q1, lambda q1, q2: (q2, q1)
         return outer, inner, i, j, lambda q1, q2: q1 * inner + q2, lambda q1, q2: (q1, q2)
 
@@ -143,6 +154,28 @@
         n1, n2, p1, p2, slot_of, place = route(k)
         send(k, slot, n1 - 1 + p2, cond & (p2 + 1 < n2), *place(p1, p2 + 1))
         send(k, slot, n1 - 2 + p2, cond & (p2 - 1 >= 0), *place(p1, p2 - 1))
+
+    def central(row):
+        return (row >= middle[0]) & (row <= middle[1])
+
+    def turn(k):
+        slot = i * inner + 1 - j
+        wait_blocks(k, 0, 1, central(i), m_recv.at[outer])
+        send(k, slot, 0, central(i) & (i + 1 < outer), i + 1, j, m_recv.at[i])
+        send(k, slot, 0, central(i) & (i > 0), i - 1, j, m_recv.at[i])
+
+    def pass_on(k, u, closing):
+        for step in (-1, 1):
+            origin = i + step * u
+            valid = (origin >= 0) & (origin < outer) & central(origin)
+            origin = jnp.clip(origin, 0, outer - 1)
+            onward = i - step
+            passed = (onward >= 0) & (onward < outer)
+            if closing:
+                wait_blocks(k, 0, 1, valid & ~passed, m_recv.at[origin])
+            else:
+                wait_blocks(k, 0, 1, valid & passed, m_recv.at[origin])
+                send(k, origin * inner + 1 - j, 0, valid & passed, onward, j, m_recv.at[origin])
 
     def own(k):
         n1, n2, p1, p2, slot_of, place = route(k)
@@ -151,7 +184,11 @@
             pltpu.make_async_copy(block, block, load_x.at[k // GROUP]).wait()
         send(k, tp, p1, p1 + 1 < n1, *place(p1 + 1, p2))
         send(k, tp, p1 - 1, p1 - 1 >= 0, *place(p1 - 1, p2))
-        cross(k, tp, p1 >= 0)
+        if k == mixed:
+            send(k, tp, 0, central(i), i, 1 - j, m_recv.at[outer])
+            cross(k, tp, ~central(i))
+        else:
+            cross(k, tp, p1 >= 0)
 
     def line(k, t):
         n1, n2, p1, p2, slot_of, place = route(k)
@@ -164,27 +201,34 @@
             wait_blocks(k, mark, 1, valid)
             onward = p1 - step
             send(k, slot, mark, valid & (onward >= 0) & (onward < n1), *place(onward, p2))
-            cross(k, slot, valid)
-
-    def second_line(k, u):
+            cross(k, slot, valid & ~central(origin) if k == mixed else valid)
+
+    def second_line(k, u, closing):
         n1, n2, p1, p2, slot_of, place = route(k)
         for step in (-1, 1):
             origin = p2 + step * u
             valid = (origin >= 0) & (origin < n2)
             origin = jnp.clip(origin, 0, n2 - 1)
             mark = n1 - 1 + jnp.clip(origin - (step > 0), 0, n2 - 2)
-            wait_blocks(k, mark, n1, valid)
             onward = p2 - step
-            if n2 > 2:
+            passed = (onward >= 0) & (onward < n2) if n2 > 2 else False
+            if closing:
+                count = n1 - len(middle) if k == mixed else n1
+                wait_blocks(k, mark, count, valid & ~passed if n2 > 2 else valid)
+            elif n2 > 2:
+                wait_blocks(k, mark, n1, valid & passed)
                 for r in range(n1):
                     slot = slot_of((p1 + r) % n1, origin)
-                    send(k, slot, mark, valid & (onward >= 0) & (onward < n2), *place(p1, onward))
+                    send(k, slot, mark, valid & passed, *place(p1, onward))
 
     def drain(at_i, at_j):
         totals = [0] * -(-units // BATCH)
         for k in range(units):
-            n1, n2, p1, p2 = (inner, outer, at_j, at_i) if k in SWAPPED else (outer, inner, at_i, at_j)
+            n1, n2, p1, p2 = (inner, outer, at_j, at_i) if k in swapped else (outer, inner, at_i, at_j)
             count = n1 * ((p2 + 1 < n2) + (p2 > 0))
+            if k == mixed:
+                count -= sum(m != p1 for m in middle)
+                count += sum((p1 + 1 < n1) * (m <= p1) + (p1 > 0) * (m >= p1) for m in middle)
             count += (1 + p1) * (p1 + 1 < n1) + (n1 - p1) * (p1 > 0)
             count += n1 * (p2 * (p2 + 1 < n2) + (n2 - 1 - p2) * (p2 > 0))
             totals[k // BATCH] += count
@@ -240,27 +284,36 @@
         elif kind == "line":
             line(k, t)
         elif kind == "cross":
-            second_line(k, t)
+            second_line(k, t, False)
+        elif kind == "turn":
+            turn(k)
+        elif kind == "pass":
+            pass_on(k, t, False)
         else:
             if not loaded:
                 pltpu.make_async_copy(cot, cot, load_g).wait()
                 loaded = True
+            for u in range(1, route(k)[1]):
+                second_line(k, u, True)
+            if k == mixed:
+                for u in range(1, outer):
+                    pass_on(k, u, True)
             consume(k)
             if k == units - 2:
                 for h in range(per_segment - 1):
                     sums = inner_products(h, sums)
     sums = inner_products(per_segment - 1, sums)
-    lane = lax.broadcasted_iota(jnp.int32, (SUBLANES, LANES), 1)
-    packed = jnp.zeros((SUBLANES, LANES), jnp.float32)
+    lane = lax.broadcasted_iota(jnp.int32, (1, LANES), 1)
+    packed = jnp.zeros((1, LANES), jnp.float32)
     for n, total in enumerate(sums):
-        packed = jnp.where(lane == n, jnp.sum(total, axis=1, keepdims=True), packed)
+        packed = jnp.where(lane == n, jnp.sum(total, keepdims=True), packed)
     tile_tp[0] = packed
     for d in range(peers - 1, -1, -1):
         for s in range(replicas - 1, -1, -1):
             if d or s:
                 pltpu.make_async_remote_copy(
                     tile_tp.at[0], tile_tp.at[s * peers + d], t_send, t_recv,
-                    device_id=(rep ^ s, (tp + d) % peers), device_id_type=MESH,
+                    device_id=(rep ^ s, tp ^ d), device_id_type=MESH,
                 ).start()
     pltpu.make_async_copy(states, states, load_s).wait()
     others = tile_tp.at[pl.ds(1, replicas * peers - 1)]
@@ -268,10 +321,7 @@
     index = {pair: n for n, pair in enumerate(pairs)}
     seen = []
     for s in range(replicas):
-        total = tile_tp[s * peers]
-        for d in range(1, peers):
-            total = total + tile_tp[s * peers + d]
-        seen.append(total)
+        seen.append(jnp.sum(tile_tp[pl.ds(s * peers, peers)], axis=0))
     gram = {}
     for s, t in pairs:
         value = None
@@ -298,7 +348,7 @@
     def w_send_start(step, s, q):
         m = masks[step]
         pltpu.make_async_remote_copy(
-            w_at(s, q), w_at(s, q), w_send, w_last if step == last else w_recv.at[s ^ m, q],
+            w_at(s, q), w_at(s, q), w_send, w_last if step == last else w_recv.at[(s ^ m) // 2, q],
             device_id=(rep ^ m, tp), device_id_type=MESH,
         ).start()
 
@@ -326,7 +376,7 @@
         for step in range(len(masks)):
             w_send_start(step, 0, q)
     def relay(q, step, s):
-        pltpu.make_async_copy(w_at(s, q), w_at(s, q), w_recv.at[s, q]).wait()
+        pltpu.make_async_copy(w_at(s, q), w_at(s, q), w_recv.at[s // 2, q]).wait()
         for later in range(step + 1, len(masks)):
             w_send_start(later, s, q)
 
@@ -351,15 +401,13 @@
 
 def deliver(*refs):
     sources, targets, sem = refs[:5], refs[5:10], refs[10]
-    moves = []
     for n, (src, dst) in enumerate(zip(sources, targets)):
         step = src.shape[0] // PIECES
         for q in range(PIECES):
             at = pl.ds(q * step, step)
-            moves.append(pltpu.make_async_copy(src.at[at], dst.at[at], sem.at[n, q]))
-            moves[-1].start()
-    for move in moves:
-        move.wait()
+            pltpu.make_async_copy(src.at[at], dst.at[at], sem.at[n]).start()
+    for n, (src, dst) in enumerate(zip(sources, targets)):
+        pltpu.make_async_copy(src, dst, sem.at[n]).wait()
 
 
 def per_device(inputs, cotangent, master, moment, second):
@@ -389,18 +437,19 @@
             pltpu.VMEM((replicas - 1, rows, features), jnp.float32),
             pltpu.VMEM((replicas, rows, features), jnp.float32),
             pltpu.VMEM((3, rows, features), jnp.float32),
-            pltpu.VMEM((replicas * peers, SUBLANES, LANES), jnp.float32),
+            pltpu.VMEM((replicas * peers, 1, LANES), jnp.float32),
             dma((-(-units // GROUP),)),
             dma(()),
             dma(()),
             dma((-(-units // BATCH),)),
             dma((units, outer + inner - 2)),
+            dma((outer + 1,)),
             dma(()),
             dma((per_segment,)),
             dma(()),
             dma(()),
             dma(()),
-            dma((replicas, PIECES)),
+            dma((replicas // 2, PIECES)),
             dma(()),
         ],
         compiler_params=pltpu.CompilerParams(
@@ -414,7 +463,7 @@
         out_shape=tuple(jax.ShapeDtypeStruct(r.shape, r.dtype) for r in results),
         in_specs=[vmem] * 5,
         out_specs=(anywhere,) * 5,
-        scratch_shapes=[dma((5, PIECES))],
+        scratch_shapes=[dma((5,))],
         compiler_params=pltpu.CompilerParams(vmem_limit_bytes=1024 * 1024),
         name="deliver",
     )(*results)

time: 112 us -> 111 us (level)
  Pallas kernels: 112 us -> 110 us
    pallas_call x1, Pallas kernels: 109 us -> 107 us  [per_device(): pl.pallas_call(functools.partial(kernel, replicas, outer, inner), out_sha...]
where the time goes in v3:
time: 111 us
  Pallas kernels  110 us (99%)
    pallas_call x1, Pallas kernels, per_device(): pl.pallas_call(functools.partial(kernel, replicas, outer, inner), out_sha...  107 us
    pallas_call x1, Pallas kernels, per_device(): pl.pallas_call(deliver, out_shape=tuple((jax.ShapeDtypeStruct(r.shape, r....  2.67 us

profile of v3, /device:TPU:0, one launch (start us, length us, event | category | flops | bytes accessed | tf_op | source)
XLA Modules:
  0.0 110.6 jit_solution(10371117383270297743)
XLA Ops:
  0.6 107.3 %adasum_adam.1 = (f32[256,1024]{1,0:T(8,128)S(1)}, f32[256,1024]{1,0:T(8,128)S(1)}, f32[256,1024]{1,0:T(8,128)S(1)}, f32[256,1024]{1,0:T(8,128)S(1)}, bf16[1024,1024]{1,0:T(8,128)(2,1)S(1)}) custom-call(bf16[512,1024]{1,0:T(8,128)(2,1)} %x_hbm.1, bf16[4096,1024]{1,0:T(8,128)(2,1)} %g_hbm.1, f32[256,1024]{1,0:T(8,128)} %master_hbm.1, f32[256,1024]{1,0:T(8,128)} %moment_hbm.1, ...), custom_call_target="tpu_custom_call" | custom-call | tf_op jit(solution)/shard_map/adasum_adam/pallas_call | solution.py:429
  108.0 2.7 %deliver.1 = (f32[256,1024]{1,0:T(8,128)}, f32[256,1024]{1,0:T(8,128)}, f32[256,1024]{1,0:T(8,128)}, f32[256,1024]{1,0:T(8,128)}, bf16[1024,1024]{1,0:T(8,128)(2,1)}) custom-call(f32[256,1024]{1,0:T(8,128)S(1)} %get-tuple-element.10.refs_0_, f32[256,1024]{1,0:T(8,128)S(1)} %get-tuple-element.11.refs_1_, f32[256,1024]{1,0:T(8,128)S(1)} %get-tuple-element.12.refs_2_, ...), custom_call_target="tpu_custom_call" | custom-call | tf_op jit(solution)/shard_map/deliver/pallas_call | solution.py:461

commit v4 on v3

--- a/solution.py
+++ b/solution.py
@@ -16,15 +16,15 @@
 SUBLANES = 8
 PIECES = 8
 SPLIT = 2
-OWN_LEAD = 9
+OWN_LEAD = 7
 LINE_LEAD = (4.5, 3.5, 2.5)
-SWAP_LEAD = (7.0,)
+SWAP_LEAD = (4.5,)
 LINE_CROSS = (0,)
-SWAP_CROSS = (4.0, 2.0, 1.5)
-SWAPPED = (5, 14)
+SWAP_CROSS = (2.0, 1.5, 1.5)
+SWAPPED = (9, 14)
 GROUP = 4
 BATCH = 8
-MIXED = 11
+MIXED = (4, 11)
 MESH = pl.DeviceIdType.MESH
 
 
@@ -54,8 +54,8 @@
 def timeline(units, outer, inner):
     steps = []
     for k in range(units):
-        mixed = k == MIXED and inner == 2
-        swap = not mixed and k in SWAPPED + (MIXED,)
+        mixed = k in MIXED and inner == 2
+        swap = not mixed and k in SWAPPED + MIXED
         n1, n2 = (inner, outer) if swap else (outer, inner)
         steps.append((k - OWN_LEAD, 0, "own", k, 0))
         lead = SWAP_LEAD if swap else LINE_LEAD
@@ -90,9 +90,9 @@
     i, j = tp // inner, tp % inner
     units = xg.shape[0] // peers
     tokens, width = xg.shape[1], xg.shape[2]
-    swapped = SWAPPED if inner == 2 else SWAPPED + (MIXED,)
-    mixed = MIXED if inner == 2 else units
-    middle = (outer // 2 - 1, outer // 2)
+    swapped = SWAPPED if inner == 2 else SWAPPED + MIXED
+    mixed = MIXED if inner == 2 else ()
+    edges = (0, outer - 1)
     chunks = units // SPLIT
     per_segment = chunks // replicas
     segment_order = list(range(replicas - 1, -1, -1))
@@ -155,27 +155,27 @@
         send(k, slot, n1 - 1 + p2, cond & (p2 + 1 < n2), *place(p1, p2 + 1))
         send(k, slot, n1 - 2 + p2, cond & (p2 - 1 >= 0), *place(p1, p2 - 1))
 
-    def central(row):
-        return (row >= middle[0]) & (row <= middle[1])
+    def at_edge(row):
+        return (row == edges[0]) | (row == edges[1])
 
     def turn(k):
         slot = i * inner + 1 - j
-        wait_blocks(k, 0, 1, central(i), m_recv.at[outer])
-        send(k, slot, 0, central(i) & (i + 1 < outer), i + 1, j, m_recv.at[i])
-        send(k, slot, 0, central(i) & (i > 0), i - 1, j, m_recv.at[i])
+        wait_blocks(k, 0, 1, at_edge(i), m_recv.at[mixed.index(k), outer])
+        send(k, slot, 0, at_edge(i) & (i + 1 < outer), i + 1, j, m_recv.at[mixed.index(k), i])
+        send(k, slot, 0, at_edge(i) & (i > 0), i - 1, j, m_recv.at[mixed.index(k), i])
 
     def pass_on(k, u, closing):
         for step in (-1, 1):
             origin = i + step * u
-            valid = (origin >= 0) & (origin < outer) & central(origin)
+            valid = (origin >= 0) & (origin < outer) & at_edge(origin)
             origin = jnp.clip(origin, 0, outer - 1)
             onward = i - step
             passed = (onward >= 0) & (onward < outer)
             if closing:
-                wait_blocks(k, 0, 1, valid & ~passed, m_recv.at[origin])
+                wait_blocks(k, 0, 1, valid & ~passed, m_recv.at[mixed.index(k), origin])
             else:
-                wait_blocks(k, 0, 1, valid & passed, m_recv.at[origin])
-                send(k, origin * inner + 1 - j, 0, valid & passed, onward, j, m_recv.at[origin])
+                wait_blocks(k, 0, 1, valid & passed, m_recv.at[mixed.index(k), origin])
+                send(k, origin * inner + 1 - j, 0, valid & passed, onward, j, m_recv.at[mixed.index(k), origin])
 
     def own(k):
         n1, n2, p1, p2, slot_of, place = route(k)
@@ -184,9 +184,9 @@
             pltpu.make_async_copy(block, block, load_x.at[k // GROUP]).wait()
         send(k, tp, p1, p1 + 1 < n1, *place(p1 + 1, p2))
         send(k, tp, p1 - 1, p1 - 1 >= 0, *place(p1 - 1, p2))
-        if k == mixed:
-            send(k, tp, 0, central(i), i, 1 - j, m_recv.at[outer])
-            cross(k, tp, ~central(i))
+        if k in mixed:
+            send(k, tp, 0, at_edge(i), i, 1 - j, m_recv.at[mixed.index(k), outer])
+            cross(k, tp, ~at_edge(i))
         else:
             cross(k, tp, p1 >= 0)
 
@@ -201,7 +201,7 @@
             wait_blocks(k, mark, 1, valid)
             onward = p1 - step
             send(k, slot, mark, valid & (onward >= 0) & (onward < n1), *place(onward, p2))
-            cross(k, slot, valid & ~central(origin) if k == mixed else valid)
+            cross(k, slot, valid & ~at_edge(origin) if k in mixed else valid)
 
     def second_line(k, u, closing):
         n1, n2, p1, p2, slot_of, place = route(k)
@@ -213,7 +213,7 @@
             onward = p2 - step
             passed = (onward >= 0) & (onward < n2) if n2 > 2 else False
             if closing:
-                count = n1 - len(middle) if k == mixed else n1
+                count = n1 - len(edges) if k in mixed else n1
                 wait_blocks(k, mark, count, valid & ~passed if n2 > 2 else valid)
             elif n2 > 2:
                 wait_blocks(k, mark, n1, valid & passed)
@@ -226,9 +226,9 @@
         for k in range(units):
             n1, n2, p1, p2 = (inner, outer, at_j, at_i) if k in swapped else (outer, inner, at_i, at_j)
             count = n1 * ((p2 + 1 < n2) + (p2 > 0))
-            if k == mixed:
-                count -= sum(m != p1 for m in middle)
-                count += sum((p1 + 1 < n1) * (m <= p1) + (p1 > 0) * (m >= p1) for m in middle)
+            if k in mixed:
+                count -= sum(m != p1 for m in edges)
+                count += sum((p1 + 1 < n1) * (m <= p1) + (p1 > 0) * (m >= p1) for m in edges)
             count += (1 + p1) * (p1 + 1 < n1) + (n1 - p1) * (p1 > 0)
             count += n1 * (p2 * (p2 + 1 < n2) + (n2 - 1 - p2) * (p2 > 0))
             totals[k // BATCH] += count
@@ -258,15 +258,19 @@
     pairs = [(s, t) for s in range(replicas) for t in range(s, replicas)]
     fold = gr.shape[2] // LANES
 
-    def inner_products(h, sums):
-        piece = gr.at[pl.ds(0, replicas - 1), pl.ds(h * width, width)]
-        pltpu.make_async_copy(piece, piece, g_recv.at[h]).wait()
+    def inner_products(h, sums, chosen, fresh=True):
+        if fresh:
+            piece = gr.at[pl.ds(0, replicas - 1), pl.ds(h * width, width)]
+            pltpu.make_async_copy(piece, piece, g_recv.at[h]).wait()
 
         def products(n, sums):
             at = pl.ds(pl.multiple_of(h * width + n * SUBLANES, SUBLANES), SUBLANES)
-            block = [gr[s, at, :] for s in range(replicas)]
+            block = {s: gr[s, at, :] for s in sorted({m for pair in chosen for m in pair})}
             out = []
             for total, (s, t) in zip(sums, pairs):
+                if (s, t) not in chosen:
+                    out.append(total)
+                    continue
                 prod = block[s] * block[t]
                 part = prod[:, :LANES]
                 for f in range(1, fold):
@@ -295,14 +299,15 @@
                 loaded = True
             for u in range(1, route(k)[1]):
                 second_line(k, u, True)
-            if k == mixed:
+            if k in mixed:
                 for u in range(1, outer):
                     pass_on(k, u, True)
             consume(k)
-            if k == units - 2:
+            if k == units - SPLIT - 1:
                 for h in range(per_segment - 1):
-                    sums = inner_products(h, sums)
-    sums = inner_products(per_segment - 1, sums)
+                    sums = inner_products(h, sums, pairs)
+                sums = inner_products(per_segment - 1, sums, [pair for pair in pairs if pair[0]])
+    sums = inner_products(per_segment - 1, sums, [pair for pair in pairs if not pair[0]], False)
     lane = lax.broadcasted_iota(jnp.int32, (1, LANES), 1)
     packed = jnp.zeros((1, LANES), jnp.float32)
     for n, total in enumerate(sums):
@@ -443,7 +448,7 @@
             dma(()),
             dma((-(-units // BATCH),)),
             dma((units, outer + inner - 2)),
-            dma((outer + 1,)),
+            dma((len(MIXED), outer + 1)),
             dma(()),
             dma((per_segment,)),
             dma(()),

time: 111 us -> 110 us (level)
  no operation moved by 1% of the time
where the time goes in v4:
time: 110 us
  Pallas kernels  109 us (99%)
    pallas_call x1, Pallas kernels, per_device(): pl.pallas_call(functools.partial(kernel, replicas, outer, inner), out_sha...  107 us
    pallas_call x1, Pallas kernels, per_device(): pl.pallas_call(deliver, out_shape=tuple((jax.ShapeDtypeStruct(r.shape, r....  2.67 us

profile of v4, /device:TPU:0, one launch (start us, length us, event | category | flops | bytes accessed | tf_op | source)
XLA Modules:
  0.0 110.1 jit_solution(2726402270523282993)
XLA Ops:
  0.6 106.6 %adasum_adam.1 = (f32[256,1024]{1,0:T(8,128)S(1)}, f32[256,1024]{1,0:T(8,128)S(1)}, f32[256,1024]{1,0:T(8,128)S(1)}, f32[256,1024]{1,0:T(8,128)S(1)}, bf16[1024,1024]{1,0:T(8,128)(2,1)S(1)}) custom-call(bf16[512,1024]{1,0:T(8,128)(2,1)} %x_hbm.1, bf16[4096,1024]{1,0:T(8,128)(2,1)} %g_hbm.1, f32[256,1024]{1,0:T(8,128)} %master_hbm.1, f32[256,1024]{1,0:T(8,128)} %moment_hbm.1, ...), custom_call_target="tpu_custom_call" | custom-call | tf_op jit(solution)/shard_map/adasum_adam/pallas_call | solution.py:434
  107.3 2.7 %deliver.1 = (f32[256,1024]{1,0:T(8,128)}, f32[256,1024]{1,0:T(8,128)}, f32[256,1024]{1,0:T(8,128)}, f32[256,1024]{1,0:T(8,128)}, bf16[1024,1024]{1,0:T(8,128)(2,1)}) custom-call(f32[256,1024]{1,0:T(8,128)S(1)} %get-tuple-element.10.refs_0_, f32[256,1024]{1,0:T(8,128)S(1)} %get-tuple-element.11.refs_1_, f32[256,1024]{1,0:T(8,128)S(1)} %get-tuple-element.12.refs_2_, ...), custom_call_target="tpu_custom_call" | custom-call | tf_op jit(solution)/shard_map/deliver/pallas_call | solution.py:466

commit v5 on v4

--- a/solution.py
+++ b/solution.py
@@ -14,7 +14,7 @@
 CORRECT_TWO = 1.0 - 0.999**50
 LANES = 128
 SUBLANES = 8
-PIECES = 8
+PIECES = 16
 SPLIT = 2
 OWN_LEAD = 7
 LINE_LEAD = (4.5, 3.5, 2.5)

time: 110 us -> 110 us (level)
  no operation moved by 1% of the time
where the time goes in v5:
time: 110 us
  Pallas kernels  109 us (99%)
    pallas_call x1, Pallas kernels, per_device(): pl.pallas_call(functools.partial(kernel, replicas, outer, inner), out_sha...  107 us
    pallas_call x1, Pallas kernels, per_device(): pl.pallas_call(deliver, out_shape=tuple((jax.ShapeDtypeStruct(r.shape, r....  2.64 us

profile of v5, /device:TPU:0, one launch (start us, length us, event | category | flops | bytes accessed | tf_op | source)
XLA Modules:
  0.0 110.1 jit_solution(5620877655758608071)
XLA Ops:
  0.6 106.7 %adasum_adam.1 = (f32[256,1024]{1,0:T(8,128)S(1)}, f32[256,1024]{1,0:T(8,128)S(1)}, f32[256,1024]{1,0:T(8,128)S(1)}, f32[256,1024]{1,0:T(8,128)S(1)}, bf16[1024,1024]{1,0:T(8,128)(2,1)S(1)}) custom-call(bf16[512,1024]{1,0:T(8,128)(2,1)} %x_hbm.1, bf16[4096,1024]{1,0:T(8,128)(2,1)} %g_hbm.1, f32[256,1024]{1,0:T(8,128)} %master_hbm.1, f32[256,1024]{1,0:T(8,128)} %moment_hbm.1, ...), custom_call_target="tpu_custom_call" | custom-call | tf_op jit(solution)/shard_map/adasum_adam/pallas_call | solution.py:434
  107.3 2.6 %deliver.1 = (f32[256,1024]{1,0:T(8,128)}, f32[256,1024]{1,0:T(8,128)}, f32[256,1024]{1,0:T(8,128)}, f32[256,1024]{1,0:T(8,128)}, bf16[1024,1024]{1,0:T(8,128)(2,1)}) custom-call(f32[256,1024]{1,0:T(8,128)S(1)} %get-tuple-element.10.refs_0_, f32[256,1024]{1,0:T(8,128)S(1)} %get-tuple-element.11.refs_1_, f32[256,1024]{1,0:T(8,128)S(1)} %get-tuple-element.12.refs_2_, ...), custom_call_target="tpu_custom_call" | custom-call | tf_op jit(solution)/shard_map/deliver/pallas_call | solution.py:466
